TPU v7x, 512 devices: a whole 4x8x8 slice. The times are simulated.
512 devices in a mesh: req: 128 (over y, z, core), tp: 4 (over x).
Axes of the slice: x: 4, y: 8, z: 8, core: 2. Of those that a mesh axis runs over, the one named last changes fastest.
Arguments:
- hidden: bfloat16 [1024, 4096], P('req'), may hold values from -512 to 512
- norm_gain: bfloat16 [4096], replicated, may hold values from 1 to 3
- lm_head: bfloat16 [4096, 131072], P(None, ('req', 'tp'))
- targets: int32 [1024], P('req'), may hold values from 0 to 131071
- segments: int32 [1024], P('req'), may hold values from 0 to 3, never falling along the last dimension, each value on 1 to 512 neighbouring positions
- scored: int32 [1024], P('req'), may hold values from 0 to 1, as said below
Outputs:
- token_logprob: float32 [1024], P('req')
- token_entropy: float32 [1024], P('req')
- seq_logprob: float32 [4], replicated
Inputs may be any that keep to these rules, and one draw needn't show every extreme that they name: At most 4 of the 8 rows of one index of req are scored, and exactly 4 on some index in every draw.
All inputs are finite; a program needn't handle non-finite values.
Results may differ from a plain program's by a relative error of at most 0.0061.
Values may be sent and summed in bfloat16 or wider, within the bound.
A program may use at most 64 MiB of HBM per device.

v0:
```python
import jax
import jax.numpy as jnp
from jax import lax
from jax.sharding import PartitionSpec as P

SEQS = 4
SCORE_MOST = 4


def local(hidden, norm_gain, lm_head, targets, segments, scored):
    col_width = lm_head.shape[1]
    own_index = lax.axis_index("req")
    first_col = (own_index * lax.axis_size("tp") + lax.axis_index("tp")) * col_width
    rank = jnp.cumsum(scored) - 1
    slots = jnp.arange(SCORE_MOST, dtype=jnp.int32)
    chosen = (scored[None, :] == 1) & (rank[None, :] == slots[:, None])
    values = jnp.sum(
        jnp.where(chosen[:, :, None], hidden.astype(jnp.float32)[None, :, :], 0.0), axis=1
    )
    row_scale = lax.rsqrt(jnp.mean(values * values, axis=1, keepdims=True) + 1e-05)
    normed = (values * row_scale * norm_gain.astype(jnp.float32)[None, :]).astype(jnp.bfloat16)
    codes = jnp.sum(jnp.where(chosen, (targets * SEQS + segments + 1)[None, :], 0), axis=1) - 1
    rows, row_codes = lax.all_gather((normed, codes), "req", axis=0, tiled=True)
    used = row_codes >= 0
    row_targets = row_codes // SEQS
    row_segments = row_codes % SEQS
    logits = jnp.dot(rows, lm_head, preferred_element_type=jnp.float32)
    own_top = jnp.max(logits, axis=1)
    scaled = jnp.exp(logits - own_top[:, None])
    own_total = jnp.sum(scaled, axis=1)
    own_weighted = jnp.sum(scaled * logits, axis=1)
    columns = first_col + jnp.arange(col_width, dtype=jnp.int32)
    own_picked = jnp.sum(jnp.where(columns[None, :] == row_targets[:, None], logits, 0.0), axis=1)
    row_top = lax.pmax(own_top, ("req", "tp"))
    factor = jnp.exp(own_top - row_top)
    sums = lax.psum(
        jnp.stack([own_total * factor, own_weighted * factor, own_picked]), ("req", "tp")
    )
    log_norm = row_top + jnp.log(sums[0])
    logprob = jnp.where(used, sums[2] - log_norm, 0.0)
    entropy = jnp.where(used, log_norm - sums[1] / sums[0], 0.0)
    seq_ids = jnp.arange(SEQS, dtype=jnp.int32)
    seq_logprob = jnp.sum(
        jnp.where(row_segments[None, :] == seq_ids[:, None], logprob[None, :], 0.0), axis=1
    )
    own = own_index * SCORE_MOST
    own_logprob = lax.dynamic_slice_in_dim(logprob, own, SCORE_MOST, 0)
    own_entropy = lax.dynamic_slice_in_dim(entropy, own, SCORE_MOST, 0)
    token_logprob = jnp.sum(jnp.where(chosen, own_logprob[:, None], 0.0), axis=0)
    token_entropy = jnp.sum(jnp.where(chosen, own_entropy[:, None], 0.0), axis=0)
    return (token_logprob, token_entropy, seq_logprob)


def solution(mesh):
    return jax.shard_map(
        local,
        mesh=mesh,
        in_specs=(P("req", None), P(), P(None, ("req", "tp")), P("req"), P("req"), P("req")),
        out_specs=(P("req"), P("req"), P()),
        check_vma=False,
    )
```

profile of v0, /device:TPU:1, one launch (start us, length us, event | category | flops | bytes accessed | tf_op | source)
XLA Modules:
  0.0 312.4 jit_solution(14411869433341832396)
XLA Ops:
  7.2 0.0 copy-start
  7.2 0.0 all-gather.3.cloned.1.call-start
  7.2 0.8 broadcast_compare_fusion.2
  8.0 0.8 reduce-window.8
  8.9 0.8 convert_element_type.9
  9.7 0.7 add_add_fusion
  10.4 0.1 select_reduce_fusion.5
  10.5 0.2 select_reduce_fusion.1
  10.7 0.1 multiply_reduce_fusion.1
  10.9 0.7 convert_element_type.10
  11.6 0.7 fusion.1
  12.3 0.0 all-gather.3.cloned.1.call-update
  12.3 1.3 dynamic-slice
  14.3 0.1 add_dynamic-update-slice_fusion
  14.4 27.8 %all-reduce = s32[512]{0:T(512)S(1)} all-reduce(s32[512]{0:T(512)S(1)} %add_dynamic-update-slice_fusion), channel_id=1, replica_groups=mesh['req'=128,'tp'=4] {'req'}, use_global_device_ids=true, to_apply=%add | all-reduce | flops 512 | bytes 4096
  42.2 60.8 %all-gather.3.cloned.1.call-done = bf16[128,4,4096]{2,1,0:T(4,128)(2,1)} async-done(((bf16[1,4,4096]{2,1,0:T(4,128)(2,1)}), bf16[128,4,4096]{2,1,0:T(4,128)(2,1)}) %all-gather.3.cloned.1.call-update) | async-done | bytes 4194320 | tf_op jit(solution)/shard_map/all_gather | solution.py:23
  103.0 6.9 %reshape.92 = bf16[512,4096]{1,0:T(8,128)(2,1)} reshape(bf16[128,4,4096]{2,1,0:T(4,128)(2,1)} %all-gather.3.cloned.1.call-done) | data formatting | bytes 8388608
  109.9 0.0 copy-done
  109.9 3.5 %fusion.7 = (f32[512]{0:T(512)S(1)}, f32[512,256]{0,1:T(8,128)S(1)}) fusion(bf16[512,4096]{1,0:T(8,128)(2,1)} %reshape.92, bf16[4096,256]{1,0:T(8,128)(2,1)S(1)} %copy-done), kind=kOutput, calls=%fused_computation.38 | convolution fusion | flops 1073872384 | bytes 6817792 | tf_op jit(solution)/shard_map/dot_general | solution.py:27
  113.4 96.0 %pmax.7 = f32[512]{0:T(512)S(1)} all-reduce(f32[512]{0:T(512)S(1)} %get-tuple-element.19), channel_id=1, replica_groups=mesh['req'=128,'tp'=4] {'req','tp'}, use_global_device_ids=true, to_apply=%region_6.7 | all-reduce | flops 512 | bytes 4096 | tf_op jit(solution)/shard_map/pmax | solution.py:34
  209.5 0.2 fusion
  209.7 94.4 %psum.7 = f32[3,512]{1,0:T(4,128)S(1)} all-reduce(f32[3,512]{1,0:T(4,128)S(1)} %pad_maximum_fusion), channel_id=1, replica_groups=mesh['req'=128,'tp'=4] {'req','tp'}, use_global_device_ids=true, to_apply=%region_9.10 | all-reduce | flops 1536 | bytes 12288 | tf_op jit(solution)/shard_map/psum | solution.py:36
  304.1 0.6 select_reduce_fusion.2
  304.8 0.1 dynamic_slice.6
  304.8 0.1 dynamic_slice.7
  304.9 0.6 select_reduce_fusion.3
  (10 shorter events, 0.1 us)
Async XLA Ops:
  7.2 102.8 %copy-start = (bf16[4096,256]{1,0:T(8,128)(2,1)S(1)}, bf16[4096,256]{1,0:T(8,128)(2,1)}, u32[]{:S(2)}) copy-start(bf16[4096,256]{1,0:T(8,128)(2,1)} %param.8) | copy-start | bytes 6291460
  7.2 95.9 %all-gather.3.cloned.1.call-start = ((), (), s32[]{:S(2)}) async-start(), calls=%async_computation | async-start | bytes 4227072 | tf_op jit(solution)/shard_map/all_gather | solution.py:23
Sparse Core Ops, SparseCore 0:
  12.4 90.5 all-gather.2
where the time goes:
time: 313 us; the launch traced here: 312 us
  blocking collectives  218 us (70%)
  waiting for transfers between devices  60.9 us (19%)
  between operations  14.7 us (5%)
  local copies, waits for them, and re-layouts  8.34 us (3%)
  other arithmetic  6.62 us (2%)
  matrix products  3.49 us (1%)
    pmax x1, blocking collectives, local(): row_top = lax.pmax(own_top, ('req', 'tp'))  96 us
    psum x1, blocking collectives, local(): lax.psum(jnp.stack([own_total * factor, own_weighted * factor, own_picked...  94.4 us
    all_gather x1, waiting for transfers between devices, local(): rows, row_codes = lax.all_gather((normed, codes), 'req', axis=0, tiled=True)  60.8 us
    unnamed x1, blocking collectives  27.8 us
    unnamed x5, local copies, waits for them, and re-layouts  8.19 us
  transfers between devices with their start and end apart: 1, of which 1 were waited for; matrix products, arithmetic and copies ran while one was open for 0% of the time, Pallas kernels for 0%

commit v1 on v0

--- a/solution.py
+++ b/solution.py
@@ -33,9 +33,9 @@
     own_picked = jnp.sum(jnp.where(columns[None, :] == row_targets[:, None], logits, 0.0), axis=1)
     row_top = lax.pmax(own_top, ("req", "tp"))
     factor = jnp.exp(own_top - row_top)
-    sums = lax.psum(
-        jnp.stack([own_total * factor, own_weighted * factor, own_picked]), ("req", "tp")
-    )
+    block = jnp.stack([own_total * factor, own_weighted * factor, own_picked])
+    pieces = lax.all_gather(block, ("req", "tp"), axis=0, tiled=False)
+    sums = pieces.sum(axis=0)
     log_norm = row_top + jnp.log(sums[0])
     logprob = jnp.where(used, sums[2] - log_norm, 0.0)
     entropy = jnp.where(used, log_norm - sums[1] / sums[0], 0.0)

time: 313 us -> 336 us (1.073)
  waiting for transfers between devices: 60.9 us -> 175 us
  blocking collectives: 218 us -> 124 us
  other arithmetic: 6.62 us -> 10 us
    all_gather x0 -> x1, waiting for transfers between devices: none -> 114 us  [local(): pieces = lax.all_gather(block, ('req', 'tp'), axis=0, tiled=False)]
    psum x1 -> x0, blocking collectives: 94.4 us -> none  [local(): lax.psum(jnp.stack([own_total * factor, own_weighted * factor, own_picked...]
  transfers between devices with their start and end apart: 1 -> 2, of which waited for: 1 -> 2; matrix products, arithmetic and copies ran while one was open for 0% -> 0% of each run, Pallas kernels for 0% -> 0%
where the time goes in v1:
time: 336 us; the launch traced here: 335 us
  waiting for transfers between devices  175 us (52%)
  blocking collectives  124 us (37%)
  between operations  14.8 us (4%)
  other arithmetic  10 us (3%)
  local copies, waits for them, and re-layouts  8.34 us (2%)
  matrix products  3.49 us (1%)
    all_gather x1, waiting for transfers between devices, local(): pieces = lax.all_gather(block, ('req', 'tp'), axis=0, tiled=False)  114 us
    pmax x1, blocking collectives, local(): row_top = lax.pmax(own_top, ('req', 'tp'))  96 us
    all_gather x1, waiting for transfers between devices, local(): rows, row_codes = lax.all_gather((normed, codes), 'req', axis=0, tiled=True)  60.8 us
    unnamed x1, blocking collectives  27.8 us
    unnamed x5, local copies, waits for them, and re-layouts  8.19 us
  transfers between devices with their start and end apart: 2, of which 2 were waited for; matrix products, arithmetic and copies ran while one was open for 0% of the time, Pallas kernels for 0%

profile of v1, /device:TPU:1, one launch (start us, length us, event | category | flops | bytes accessed | tf_op | source)
XLA Modules:
  0.0 335.3 jit_solution(6106553528553639565)
XLA Ops:
  7.2 0.0 copy-start
  7.2 0.0 all-gather.6.cloned.1.call-start
  7.2 0.8 broadcast_compare_fusion.2
  8.0 0.8 reduce-window.8
  8.9 0.8 convert_element_type.9
  9.7 0.7 add_add_fusion
  10.4 0.1 select_reduce_fusion.5
  10.5 0.2 select_reduce_fusion.1
  10.7 0.1 multiply_reduce_fusion.1
  10.9 0.7 convert_element_type.10
  11.6 0.7 fusion.1
  12.3 0.0 all-gather.6.cloned.1.call-update
  12.3 0.0 all-gather.8.cloned.1.call-start
  12.4 1.3 dynamic-slice
  14.3 0.1 add_dynamic-update-slice_fusion
  14.4 27.8 %all-reduce = s32[512]{0:T(512)S(1)} all-reduce(s32[512]{0:T(512)S(1)} %add_dynamic-update-slice_fusion), channel_id=1, replica_groups=mesh['req'=128,'tp'=4] {'req'}, use_global_device_ids=true, to_apply=%add | all-reduce | flops 512 | bytes 4096
  42.3 60.8 %all-gather.6.cloned.1.call-done = bf16[128,4,4096]{2,1,0:T(4,128)(2,1)} async-done(((bf16[1,4,4096]{2,1,0:T(4,128)(2,1)}), bf16[128,4,4096]{2,1,0:T(4,128)(2,1)}) %all-gather.6.cloned.1.call-update) | async-done | bytes 4194320 | tf_op jit(solution)/shard_map/all_gather | solution.py:23
  103.0 6.9 %reshape.93 = bf16[512,4096]{1,0:T(8,128)(2,1)} reshape(bf16[128,4,4096]{2,1,0:T(4,128)(2,1)} %all-gather.6.cloned.1.call-done) | data formatting | bytes 8388608
  109.9 0.0 copy-done
  109.9 3.5 %fusion.7 = (f32[512]{0:T(512)S(1)}, f32[512,256]{0,1:T(8,128)S(1)}) fusion(bf16[512,4096]{1,0:T(8,128)(2,1)} %reshape.93, bf16[4096,256]{1,0:T(8,128)(2,1)S(1)} %copy-done), kind=kOutput, calls=%fused_computation.38 | convolution fusion | flops 1073872384 | bytes 6817792 | tf_op jit(solution)/shard_map/dot_general | solution.py:27
  113.4 96.0 %pmax.7 = f32[512]{0:T(512)S(1)} all-reduce(f32[512]{0:T(512)S(1)} %get-tuple-element.19), channel_id=1, replica_groups=mesh['req'=128,'tp'=4] {'req','tp'}, use_global_device_ids=true, to_apply=%region_6.7 | all-reduce | flops 512 | bytes 4096 | tf_op jit(solution)/shard_map/pmax | solution.py:34
  209.5 0.2 fusion
  209.7 0.6 maximum_bitcast_fusion
  210.3 0.0 all-gather.8.cloned.1.call-update
  210.3 113.9 %all-gather.8.cloned.1.call-done = f32[512,3,512]{2,1,0:T(4,128)} async-done(((f32[1,3,512]{2,1,0:T(4,128)}), f32[512,3,512]{2,1,0:T(4,128)}) %all-gather.8.cloned.1.call-update) | async-done | bytes 3145744 | tf_op jit(solution)/shard_map/all_gather | solution.py:37
  324.2 2.8 reduce_sum.96
  327.1 0.6 select_reduce_fusion.2
  327.7 0.1 dynamic_slice.6
  327.8 0.1 dynamic_slice.7
  327.8 0.6 select_reduce_fusion.3
  (9 shorter events, 0.1 us)
Async XLA Ops:
  7.2 102.8 %copy-start = (bf16[4096,256]{1,0:T(8,128)(2,1)S(1)}, bf16[4096,256]{1,0:T(8,128)(2,1)}, u32[]{:S(2)}) copy-start(bf16[4096,256]{1,0:T(8,128)(2,1)} %param.8) | copy-start | bytes 6291460
  7.2 95.9 %all-gather.6.cloned.1.call-start = ((), (), s32[]{:S(2)}) async-start(), calls=%async_computation | async-start | bytes 4227072 | tf_op jit(solution)/shard_map/all_gather | solution.py:23
  12.3 311.9 %all-gather.8.cloned.1.call-start = ((), (), s32[]{:S(2)}) async-start(), calls=%async_computation.1 | async-start | bytes 4202496 | tf_op jit(solution)/shard_map/all_gather | solution.py:37
Sparse Core Ops, SparseCore 0:
  12.4 90.5 all-gather.5
  210.4 113.7 all-gather.7
